TPU v7x, 32 devices: a whole 2x2x4 slice. The times are simulated.
32 devices in a mesh: shard: 16 (over z, x, core), replica: 2 (over y).
Axes of the slice: x: 2, y: 2, z: 4, core: 2. Of those that a mesh axis runs over, the one named last changes fastest.
Arguments:
- tokens: float32 [4096, 1024], P(('shard', 'replica')), may hold values from -6 to 6
- segment_ids: int32 [32, 128], P(('shard', 'replica')), may hold values from 0 to 3, never falling along the last dimension, each value on 1 to 64 neighbouring positions
- cotangent: float32 [4096, 1024], P(('shard', 'replica')), may hold values from -6 to 6
- norm1_gain: bfloat16 [1024], P('shard'), may hold values from 0.099609375 to 1.8984375
- norm1_shift: bfloat16 [1024], P('shard'), may hold values from -3 to 3
- qkv_weight: bfloat16 [1024, 3072], P('shard'), may hold values from -0.1875 to 0.1875
- query_bias: bfloat16 [1024], P('shard'), may hold values from -3 to 3
- value_bias: bfloat16 [1024], P('shard'), may hold values from -3 to 3
- out_weight: bfloat16 [1024, 1024], P('shard'), may hold values from -0.75 to 0.75
- out_bias: bfloat16 [1024], P('shard'), may hold values from -3 to 3
- norm2_gain: bfloat16 [1024], P('shard'), may hold values from 0.099609375 to 1.8984375
- norm2_shift: bfloat16 [1024], P('shard'), may hold values from -3 to 3
- fc_weight: bfloat16 [1024, 4096], P('shard'), may hold values from -0.1875 to 0.1875
- fc_bias: bfloat16 [4096], P('shard'), may hold values from -3 to 3
- proj_weight: bfloat16 [4096, 1024], P('shard'), may hold values from -0.09375 to 0.09375
- proj_bias: bfloat16 [1024], P('shard'), may hold values from -3 to 3
Outputs:
- output: float32 [4096, 1024], P(('shard', 'replica'))
- tokens_grad: float32 [4096, 1024], P(('shard', 'replica'))
- norm1_gain_grad: float32 [1024], P('shard')
- norm1_shift_grad: float32 [1024], P('shard')
- qkv_weight_grad: float32 [1024, 3072], P('shard')
- query_bias_grad: float32 [1024], P('shard')
- value_bias_grad: float32 [1024], P('shard')
- out_weight_grad: float32 [1024, 1024], P('shard')
- out_bias_grad: float32 [1024], P('shard')
- norm2_gain_grad: float32 [1024], P('shard')
- norm2_shift_grad: float32 [1024], P('shard')
- fc_weight_grad: float32 [1024, 4096], P('shard')
- fc_bias_grad: float32 [4096], P('shard')
- proj_weight_grad: float32 [4096, 1024], P('shard')
- proj_bias_grad: float32 [1024], P('shard')
Inputs may be any that keep to these rules, and one draw needn't show every extreme that they name: `segment_ids`: in each row (one device's tokens) the numbers never fall, every number from 0 to 3 occurs as one run of 1 to 64 positions, and one run holds exactly 64.
All inputs are finite; a program needn't handle non-finite values.
Results may differ from a plain program's by a relative error of at most 0.012.
Values may be sent and summed in bfloat16 or wider, within the bound.
A program may use at most 192 MiB of HBM per device.

v0:
```python
import jax
import jax.numpy as jnp
from jax import lax
from jax.sharding import PartitionSpec as P

HEADS = 16
HEAD = 64
EPS = 1e-05
GELU_C = 0.7978845608028654
GELU_A = 0.044715


def layer_norm(values, gain, shift):
    row_mean = jnp.mean(values, axis=-1, keepdims=True)
    centered = values - row_mean
    inv_std = lax.rsqrt(jnp.mean(centered * centered, axis=-1, keepdims=True) + EPS)
    normed = centered * inv_std
    return (normed * gain.astype(jnp.float32) + shift.astype(jnp.float32), normed, inv_std)


def norm_back(grad_out, normed, inv_std, gain):
    scaled = grad_out * gain.astype(jnp.float32)
    return inv_std * (
        scaled
        - jnp.mean(scaled, axis=-1, keepdims=True)
        - normed * jnp.mean(scaled * normed, axis=-1, keepdims=True)
    )


def gelu_pair(pre_act):
    tangent = jnp.tanh(GELU_C * (pre_act + GELU_A * pre_act * pre_act * pre_act))
    value = 0.5 * pre_act * (1.0 + tangent)
    slope = 0.5 * (1.0 + tangent) + 0.5 * pre_act * (1.0 - tangent * tangent) * GELU_C * (
        1.0 + 3.0 * GELU_A * pre_act * pre_act
    )
    return (value, slope)


def contract(left, right, left_axis, right_axis):
    return lax.dot_general(
        left, right, (((left_axis,), (right_axis,)), ((), ())), preferred_element_type=jnp.float32
    )


def masked_scores(query, keyed, segment_row, scale):
    rows = query.shape[0]
    scores = jnp.einsum("qhd,khd->hqk", query, keyed, preferred_element_type=jnp.float32) * scale
    position = jnp.arange(rows)
    allowed = (segment_row[:, None] == segment_row[None, :]) & (
        position[None, :] <= position[:, None]
    )
    return jnp.where(allowed[None], scores, -1e30)


def on_device(
    tokens,
    segment_ids,
    cotangent,
    norm1_gain,
    norm1_shift,
    qkv_weight,
    query_bias,
    value_bias,
    out_weight,
    out_bias,
    norm2_gain,
    norm2_shift,
    fc_weight,
    fc_bias,
    proj_weight,
    proj_bias,
):
    rows, width = tokens.shape
    segment_row = segment_ids[0]
    scale = HEAD ** (-0.5)
    gain1, shift1, w_qkv, bias_query, bias_value, w_out, bias_out = (
        lax.all_gather(norm1_gain, "shard", axis=0, tiled=True),
        lax.all_gather(norm1_shift, "shard", axis=0, tiled=True),
        lax.all_gather(qkv_weight, "shard", axis=0, tiled=True),
        lax.all_gather(query_bias, "shard", axis=0, tiled=True),
        lax.all_gather(value_bias, "shard", axis=0, tiled=True),
        lax.all_gather(out_weight, "shard", axis=0, tiled=True),
        lax.all_gather(out_bias, "shard", axis=0, tiled=True),
    )
    ln1, normed1, inv1 = layer_norm(tokens, gain1, shift1)
    input1 = ln1.astype(jnp.bfloat16)
    qkv_bias = jnp.concatenate(
        [
            bias_query.astype(jnp.float32),
            jnp.zeros((width,), jnp.float32),
            bias_value.astype(jnp.float32),
        ]
    )
    projected = jnp.dot(input1, w_qkv, preferred_element_type=jnp.float32) + qkv_bias
    query = projected[:, :width].reshape(rows, HEADS, HEAD).astype(jnp.bfloat16)
    keyed = projected[:, width : 2 * width].reshape(rows, HEADS, HEAD).astype(jnp.bfloat16)
    valued = projected[:, 2 * width :].reshape(rows, HEADS, HEAD).astype(jnp.bfloat16)
    scores = masked_scores(query, keyed, segment_row, scale)
    top = jnp.max(scores, axis=-1, keepdims=True)
    log_total = top + jnp.log(jnp.sum(jnp.exp(scores - top), axis=-1, keepdims=True))
    probs_low = jnp.exp(scores - log_total).astype(jnp.bfloat16)
    context = jnp.einsum("hqk,khd->qhd", probs_low, valued, preferred_element_type=jnp.float32)
    context = context.reshape(rows, width).astype(jnp.bfloat16)
    middle = (
        tokens
        + jnp.dot(context, w_out, preferred_element_type=jnp.float32)
        + bias_out.astype(jnp.float32)
    )
    gain2, shift2, w_fc, bias_fc, w_proj, bias_proj = (
        lax.all_gather(norm2_gain, "shard", axis=0, tiled=True),
        lax.all_gather(norm2_shift, "shard", axis=0, tiled=True),
        lax.all_gather(fc_weight, "shard", axis=0, tiled=True),
        lax.all_gather(fc_bias, "shard", axis=0, tiled=True),
        lax.all_gather(proj_weight, "shard", axis=0, tiled=True),
        lax.all_gather(proj_bias, "shard", axis=0, tiled=True),
    )
    ln2, normed2, inv2 = layer_norm(middle, gain2, shift2)
    input2 = ln2.astype(jnp.bfloat16)
    pre_act = jnp.dot(input2, w_fc, preferred_element_type=jnp.float32) + bias_fc.astype(
        jnp.float32
    )
    gelu_value, gelu_slope = gelu_pair(pre_act)
    activated = gelu_value.astype(jnp.bfloat16)
    output = (
        middle
        + jnp.dot(activated, w_proj, preferred_element_type=jnp.float32)
        + bias_proj.astype(jnp.float32)
    )
    grad_proj_bias = jnp.sum(cotangent, axis=0)
    cot_low = cotangent.astype(jnp.bfloat16)
    grad_pre = contract(cot_low, w_proj, 1, 1) * gelu_slope
    grad_fc_bias = jnp.sum(grad_pre, axis=0)
    grad_pre_low = grad_pre.astype(jnp.bfloat16)
    grad_fc_weight = contract(input2, grad_pre_low, 0, 0)
    grad_in2 = contract(grad_pre_low, w_fc, 1, 1)
    grad_gain2 = jnp.sum(grad_in2 * normed2, axis=0)
    grad_shift2 = jnp.sum(grad_in2, axis=0)
    grad_middle = cotangent + norm_back(grad_in2, normed2, inv2, gain2)
    grad_proj_weight = contract(activated, cot_low, 0, 0)
    (
        share_gain2,
        share_shift2,
        share_fc_weight,
        share_fc_bias,
        share_proj_weight,
        share_proj_bias,
    ) = (
        lax.psum_scatter(grad_gain2, "shard", scatter_dimension=0, tiled=True),
        lax.psum_scatter(grad_shift2, "shard", scatter_dimension=0, tiled=True),
        lax.psum_scatter(grad_fc_weight, "shard", scatter_dimension=0, tiled=True),
        lax.psum_scatter(grad_fc_bias, "shard", scatter_dimension=0, tiled=True),
        lax.psum_scatter(grad_proj_weight, "shard", scatter_dimension=0, tiled=True),
        lax.psum_scatter(grad_proj_bias, "shard", scatter_dimension=0, tiled=True),
    )
    (
        share_gain2,
        share_shift2,
        share_fc_weight,
        share_fc_bias,
        share_proj_weight,
        share_proj_bias,
    ) = lax.psum(
        (
            share_gain2,
            share_shift2,
            share_fc_weight,
            share_fc_bias,
            share_proj_weight,
            share_proj_bias,
        ),
        "replica",
    )
    grad_out_bias = jnp.sum(grad_middle, axis=0)
    mid_low = grad_middle.astype(jnp.bfloat16)
    grad_out_weight = contract(context, mid_low, 0, 0)
    grad_context = contract(mid_low, w_out, 1, 1)
    grad_context = grad_context.reshape(rows, HEADS, HEAD).astype(jnp.bfloat16)
    again_scores = masked_scores(query, keyed, segment_row, scale)
    probs = jnp.exp(again_scores - log_total)
    probs_low = probs.astype(jnp.bfloat16)
    grad_value = jnp.einsum(
        "hqk,qhd->khd", probs_low, grad_context, preferred_element_type=jnp.float32
    )
    grad_probs = jnp.einsum(
        "qhd,khd->hqk", grad_context, valued, preferred_element_type=jnp.float32
    )
    grad_scores = probs * (grad_probs - jnp.sum(probs * grad_probs, axis=-1, keepdims=True)) * scale
    grad_scores = grad_scores.astype(jnp.bfloat16)
    grad_query = jnp.einsum("hqk,khd->qhd", grad_scores, keyed, preferred_element_type=jnp.float32)
    grad_key = jnp.einsum("hqk,qhd->khd", grad_scores, query, preferred_element_type=jnp.float32)
    grad_query = grad_query.reshape(rows, width)
    grad_key = grad_key.reshape(rows, width)
    grad_value = grad_value.reshape(rows, width)
    grad_query_bias = jnp.sum(grad_query, axis=0)
    grad_value_bias = jnp.sum(grad_value, axis=0)
    grad_qkv = jnp.concatenate([grad_query, grad_key, grad_value], axis=1).astype(jnp.bfloat16)
    grad_qkv_weight = contract(input1, grad_qkv, 0, 0)
    grad_in1 = contract(grad_qkv, w_qkv, 1, 1)
    grad_gain1 = jnp.sum(grad_in1 * normed1, axis=0)
    grad_shift1 = jnp.sum(grad_in1, axis=0)
    tokens_grad = grad_middle + norm_back(grad_in1, normed1, inv1, gain1)
    (
        share_gain1,
        share_shift1,
        share_qkv_weight,
        share_query_bias,
        share_value_bias,
        share_out_weight,
        share_out_bias,
    ) = (
        lax.psum_scatter(grad_gain1, "shard", scatter_dimension=0, tiled=True),
        lax.psum_scatter(grad_shift1, "shard", scatter_dimension=0, tiled=True),
        lax.psum_scatter(grad_qkv_weight, "shard", scatter_dimension=0, tiled=True),
        lax.psum_scatter(grad_query_bias, "shard", scatter_dimension=0, tiled=True),
        lax.psum_scatter(grad_value_bias, "shard", scatter_dimension=0, tiled=True),
        lax.psum_scatter(grad_out_weight, "shard", scatter_dimension=0, tiled=True),
        lax.psum_scatter(grad_out_bias, "shard", scatter_dimension=0, tiled=True),
    )
    (
        share_gain1,
        share_shift1,
        share_qkv_weight,
        share_query_bias,
        share_value_bias,
        share_out_weight,
        share_out_bias,
    ) = lax.psum(
        (
            share_gain1,
            share_shift1,
            share_qkv_weight,
            share_query_bias,
            share_value_bias,
            share_out_weight,
            share_out_bias,
        ),
        "replica",
    )
    return (
        output,
        tokens_grad,
        share_gain1,
        share_shift1,
        share_qkv_weight,
        share_query_bias,
        share_value_bias,
        share_out_weight,
        share_out_bias,
        share_gain2,
        share_shift2,
        share_fc_weight,
        share_fc_bias,
        share_proj_weight,
        share_proj_bias,
    )


def solution(mesh):
    in_specs = (
        P(("shard", "replica"), None),
        P(("shard", "replica"), None),
        P(("shard", "replica"), None),
        P("shard"),
        P("shard"),
        P("shard", None),
        P("shard"),
        P("shard"),
        P("shard", None),
        P("shard"),
        P("shard"),
        P("shard"),
        P("shard", None),
        P("shard"),
        P("shard", None),
        P("shard"),
    )
    out_specs = (
        P(("shard", "replica"), None),
        P(("shard", "replica"), None),
        P("shard"),
        P("shard"),
        P("shard", None),
        P("shard"),
        P("shard"),
        P("shard", None),
        P("shard"),
        P("shard"),
        P("shard"),
        P("shard", None),
        P("shard"),
        P("shard", None),
        P("shard"),
    )
    return jax.shard_map(
        on_device, mesh=mesh, in_specs=in_specs, out_specs=out_specs, check_vma=False
    )
```

profile of v0, /device:TPU:0, one launch (start us, length us, event | category | flops | bytes accessed | tf_op | source)
XLA Modules:
  0.0 957.4 jit_solution(4036300594005818929)
XLA Ops:
  18.7 64.0 %all-reduce.20 = (bf16[1024]{0:T(1024)(128)(2,1)S(1)}, bf16[1024]{0:T(1024)(128)(2,1)S(1)}, bf16[1024]{0:T(1024)(128)(2,1)S(1)}, bf16[1024]{0:T(1024)(128)(2,1)S...) all-reduce(bf16[1024]{0:T(1024)(128)(2,1)S(1)} %dynamic-update-slic, ...), channel_id=1, replica_groups=mesh['shard'=16,'replica'=2] {'shard'}, use_global_device_ids=true, to_apply=%add.3 | all-reduce | flops 8192 | bytes 32768
  83.4 17.3 %all-gather = bf16[16,1,256]{2,1,0:T(2,128)(2,1)S(1)} all-gather(bf16[1,1,256]{2,1,0:T(2,128)(2,1)S(1)} %reshape.182), channel_id=1, replica_groups=mesh['shard'=16,'replica'=2] {'shard'}, dimensions={0}, use_global_device_ids=true | all-gather | bytes 8704 | tf_op jit(solution)/shard_map/all_gather | solution.py:113
  101.3 3.8 fusion.1
  106.6 11.5 %all-gather.8.cloned.1.call-done = bf16[1024,1024]{1,0:T(8,128)(2,1)} async-done(((bf16[64,1024]{1,0:T(8,128)(2,1)}), bf16[1024,1024]{1,0:T(8,128)(2,1)}) %all-gather.8.cloned.1.call-update) | async-done | bytes 2097168 | tf_op jit(solution)/shard_map/all_gather | solution.py:82
  120.4 73.5 %all-gather.10.cloned.1.call-done = bf16[1024,4096]{1,0:T(8,128)(2,1)} async-done(((bf16[64,4096]{1,0:T(8,128)(2,1)}), bf16[1024,4096]{1,0:T(8,128)(2,1)}) %all-gather.10.cloned.1.call-update) | async-done | bytes 8388624 | tf_op jit(solution)/shard_map/all_gather | solution.py:112
  193.9 6.1 convolution_add_fusion
  200.0 69.1 %all-gather.12.cloned.1.call-done = bf16[4096,1024]{1,0:T(8,128)(2,1)} async-done(((bf16[256,1024]{1,0:T(8,128)(2,1)}), bf16[4096,1024]{1,0:T(8,128)(2,1)}) %all-gather.12.cloned.1.call-update) | async-done | bytes 8388624 | tf_op jit(solution)/shard_map/all_gather | solution.py:114
  269.1 7.8 fusion.55
  277.0 3.0 multiply_reduce_fusion.1
  280.3 2.8 fusion.33
  283.4 2.4 convolution_convert_fusion.1
  289.5 2.3 fusion.49
  292.3 6.8 fusion.29
  300.5 8.2 fusion.19
  310.2 9.3 fusion.36
  319.6 34.3 %reduce-scatter.7.cloned.1.call-done = f32[64,1024]{1,0:T(8,128)} async-done(((f32[1024,1024]{1,0:T(8,128)}), f32[64,1024]{1,0:T(8,128)}) %reduce-scatter.7.cloned.1.call-update) | async-done | bytes 262160 | tf_op jit(solution)/shard_map/reduce_scatter | solution.py:216
  353.9 138.2 %reduce-scatter.5.cloned.1.call-done = f32[64,3072]{1,0:T(8,128)} async-done(((f32[1024,3072]{1,0:T(8,128)}), f32[64,3072]{1,0:T(8,128)}) %reduce-scatter.5.cloned.1.call-update) | async-done | bytes 786448 | tf_op jit(solution)/shard_map/reduce_scatter | solution.py:213
  492.2 182.4 %reduce-scatter.9.cloned.1.call-done = f32[64,4096]{1,0:T(8,128)} async-done(((f32[1024,4096]{1,0:T(8,128)}), f32[64,4096]{1,0:T(8,128)}) %reduce-scatter.9.cloned.1.call-update) | async-done | bytes 1048592 | tf_op jit(solution)/shard_map/reduce_scatter | solution.py:150
  674.6 182.3 %reduce-scatter.11.cloned.1.call-done = f32[256,1024]{1,0:T(8,128)} async-done(((f32[4096,1024]{1,0:T(8,128)}), f32[256,1024]{1,0:T(8,128)}) %reduce-scatter.11.cloned.1.call-update) | async-done | bytes 1048592 | tf_op jit(solution)/shard_map/reduce_scatter | solution.py:152
  858.3 6.0 multiply_reduce_fusion.2
  864.3 59.7 %all-reduce.17 = (f32[1024]{0:T(1024)S(1)}, f32[1024]{0:T(1024)S(1)}, f32[1024]{0:T(1024)S(1)}, f32[1024]{0:T(1024)S(1)}, f32[1024]{0:T(1024)S(1)}, /*index=5*/f...) all-reduce(f32[1024]{0:T(1024)S(1)} %get-tuple-element.17, ...), channel_id=2, replica_groups=mesh['shard'=16,'replica'=2] {'shard'}, use_global_device_ids=true, to_apply=%region_12.13.clone | all-reduce | flops 12288 | bytes 98304
  924.7 5.7 all-reduce.18
  932.6 5.7 fusion.13
  938.3 6.7 all-reduce.23.cloned.1.call-done
  (125 shorter events, 32.2 us)
Async XLA Ops:
  7.2 93.6 %copy-start.1 = (f32[128,1024]{1,0:T(8,128)S(1)}, f32[128,1024]{1,0:T(8,128)}, u32[]{:S(2)}) copy-start(f32[128,1024]{1,0:T(8,128)} %param.16) | copy-start | bytes 1572868
  7.2 93.9 %copy-start.17 = (s32[1,128]{1,0:T(1,128)S(1)}, s32[1,128]{1,0:T(1,128)}, u32[]{:S(2)}) copy-start(s32[1,128]{1,0:T(1,128)} %param.17) | copy-start | bytes 1540
  7.2 94.0 %all-gather.6.cloned.1.call-start = ((), (), s32[]{:S(2)}) async-start(), calls=%async_computation.4 | async-start | bytes 6684672 | tf_op jit(solution)/shard_map/all_gather | solution.py:79
  7.9 110.1 %all-gather.8.cloned.1.call-start = ((), (), s32[]{:S(2)}) async-start(), calls=%async_computation.5 | async-start | bytes 2228224 | tf_op jit(solution)/shard_map/all_gather | solution.py:82
  8.7 185.2 %all-gather.10.cloned.1.call-start = ((), (), s32[]{:S(2)}) async-start(), calls=%async_computation.6 | async-start | bytes 8912896 | tf_op jit(solution)/shard_map/all_gather | solution.py:112
  9.4 259.7 %all-gather.12.cloned.1.call-start = ((), (), s32[]{:S(2)}) async-start(), calls=%async_computation.7 | async-start | bytes 8912896 | tf_op jit(solution)/shard_map/all_gather | solution.py:114
  10.0 343.9 %reduce-scatter.7.cloned.1.call-start = ((), (), s32[]{:S(2)}) async-start(), calls=%async_computation.9 | async-start | bytes 4456448 | tf_op jit(solution)/shard_map/reduce_scatter | solution.py:216
  269.1 7.8 copy-start
  276.9 3.1 copy-start.4
  276.9 3.1 copy-start.8
  280.3 3.1 copy-start.3
  283.1 2.9 copy-start.7
  283.1 4.2 copy-start.12
  283.1 209.0 %reduce-scatter.5.cloned.1.call-start = ((), (), s32[]{:S(2)}) async-start(), calls=%async_computation.8 | async-start | bytes 13369344 | tf_op jit(solution)/shard_map/reduce_scatter | solution.py:213
  285.8 3.6 copy-start.10
  289.5 9.7 %copy-start.15 = (bf16[16,64,128]{2,1,0:T(8,128)(2,1)}, bf16[16,64,128]{2,1,0:T(8,128)(2,1)S(1)}, u32[]{:S(2)}) copy-start(bf16[16,64,128]{2,1,0:T(8,128)(2,1)S(1)} %convolution_convert_fusion) | copy-start | bytes 786436
  291.8 7.4 copy-start.16
  299.2 1.3 copy-start.5
  299.2 375.4 %reduce-scatter.9.cloned.1.call-start = ((), (), s32[]{:S(2)}) async-start(), calls=%async_computation.10 | async-start | bytes 17825792 | tf_op jit(solution)/shard_map/reduce_scatter | solution.py:150
  308.6 1.6 copy-start.2
  308.7 548.2 %reduce-scatter.11.cloned.1.call-start = ((), (), s32[]{:S(2)}) async-start(), calls=%async_computation.11 | async-start | bytes 17825792 | tf_op jit(solution)/shard_map/reduce_scatter | solution.py:152
  319.6 625.5 %all-reduce.23.cloned.1.call-start = ((), (), s32[]{:S(2)}) async-start(), calls=%async_computation.12 | async-start | bytes 6291456 | tf_op jit(solution)/shard_map/psum | solution.py:227
  945.0 3.9 copy-start.14
  945.0 4.9 copy-start.13
  (3 other events, 3.1 us)
Sparse Core Ops, SparseCore 0:
  10.3 65.4 all-gather.5
  78.0 40.0 all-gather.7
  120.2 73.6 all-gather.9
  195.9 73.1 all-gather.11
  283.2 70.6 reduce-scatter.6
  358.4 133.7 reduce-scatter.4
  496.8 177.7 reduce-scatter.8
  679.3 177.5 reduce-scatter.10
  859.5 85.5 all-reduce.22
where the time goes:
time: 958 us; the launch traced here: 957 us
  waiting for transfers between devices  701 us (73%)
  blocking collectives  147 us (15%)
  matrix products  71 us (7%)
  local copies, waits for them, and re-layouts  18.9 us (2%)
  between operations  16.3 us (2%)
    reduce_scatter x1, waiting for transfers between devices, on_device(): lax.psum_scatter(grad_fc_weight, 'shard', scatter_dimension=0, tiled=True)  182 us
    reduce_scatter x1, waiting for transfers between devices, on_device(): lax.psum_scatter(grad_proj_weight, 'shard', scatter_dimension=0, tiled=True)  182 us
    reduce_scatter x1, waiting for transfers between devices, on_device(): lax.psum_scatter(grad_qkv_weight, 'shard', scatter_dimension=0, tiled=True)  138 us
    unnamed x2, blocking collectives  124 us
    all_gather x1, waiting for transfers between devices, on_device(): lax.all_gather(fc_weight, 'shard', axis=0, tiled=True)  73.5 us
    all_gather x1, waiting for transfers between devices, on_device(): lax.all_gather(proj_weight, 'shard', axis=0, tiled=True)  69.1 us
    dot_general x8, matrix products, contract(): lax.dot_general(left, right, (((left_axis,), (right_axis,)), ((), ())), p...  46.3 us
    reduce_scatter x1, waiting for transfers between devices, on_device(): lax.psum_scatter(grad_out_weight, 'shard', scatter_dimension=0, tiled=True)  34.3 us
  transfers between devices with their start and end apart: 9, of which 8 were waited for; matrix products, arithmetic and copies ran while one was open for 7% of the time, Pallas kernels for 0%

commit v1 on v0

--- a/solution.py
+++ b/solution.py
@@ -2,12 +2,26 @@
 import jax.numpy as jnp
 from jax import lax
 from jax.sharding import PartitionSpec as P
+from jax.lax import axis_index, axis_size, ppermute
 
 HEADS = 16
 HEAD = 64
 EPS = 1e-05
 GELU_C = 0.7978845608028654
 GELU_A = 0.044715
+
+
+def _produce_kinds(inner_x, in_dim):
+    along_axis = "shard"
+    field_out, prior = (axis_size(along_axis), axis_index(along_axis))
+    s_next, a_next = (inner_x, 1)
+    while a_next < field_out:
+        clean = ppermute(s_next, along_axis, list(map(lambda p: (p, p ^ a_next), range(field_out))))
+        res = jnp.concatenate([s_next, clean], axis=in_dim)
+        y2 = jnp.concatenate([clean, s_next], axis=in_dim)
+        s_next = jnp.where(prior & a_next == 0, res, y2)
+        a_next = 2 * a_next
+    return s_next
 
 
 def layer_norm(values, gain, shift):
@@ -111,7 +125,7 @@
         lax.all_gather(norm2_shift, "shard", axis=0, tiled=True),
         lax.all_gather(fc_weight, "shard", axis=0, tiled=True),
         lax.all_gather(fc_bias, "shard", axis=0, tiled=True),
-        lax.all_gather(proj_weight, "shard", axis=0, tiled=True),
+        _produce_kinds(proj_weight, 0),
         lax.all_gather(proj_bias, "shard", axis=0, tiled=True),
     )
     ln2, normed2, inv2 = layer_norm(middle, gain2, shift2)

time: 958 us -> 1090 us (1.14)
  blocking collectives: 147 us -> 323 us
  waiting for transfers between devices: 701 us -> 643 us
    unnamed x2, blocking collectives: 124 us -> 299 us
    ppermute x0 -> x4, waiting for transfers between devices: none -> 102 us  [_produce_kinds(): ppermute(s_next, along_axis, list(map(lambda p: (p, p ^ a_next), range(fi...]
    all_gather x1, waiting for transfers between devices: 73.5 us -> 0.02 us  [on_device(): lax.all_gather(fc_weight, 'shard', axis=0, tiled=True)]
    all_gather x1 -> x0, waiting for transfers between devices: 69.1 us -> none  [on_device(): lax.all_gather(proj_weight, 'shard', axis=0, tiled=True)]
    all_gather x1, waiting for transfers between devices: 11.5 us -> 0.02 us  [on_device(): lax.all_gather(out_weight, 'shard', axis=0, tiled=True)]
  transfers between devices with their start and end apart: 9 -> 12, of which waited for: 8 -> 8; matrix products, arithmetic and copies ran while one was open for 7% -> 7% of each run, Pallas kernels for 0% -> 0%
where the time goes in v1:
time: 1090 us
  waiting for transfers between devices  643 us (59%)
  blocking collectives  323 us (30%)
  matrix products  75 us (7%)
  between operations  16.7 us (2%)
  local copies, waits for them, and re-layouts  14.1 us (1%)
  other arithmetic  13.7 us (1%)
    unnamed x2, blocking collectives  299 us
    reduce_scatter x1, waiting for transfers between devices, on_device(): lax.psum_scatter(grad_proj_weight, 'shard', scatter_dimension=0, tiled=True)  182 us
    reduce_scatter x1, waiting for transfers between devices, on_device(): lax.psum_scatter(grad_fc_weight, 'shard', scatter_dimension=0, tiled=True)  182 us
    reduce_scatter x1, waiting for transfers between devices, on_device(): lax.psum_scatter(grad_qkv_weight, 'shard', scatter_dimension=0, tiled=True)  138 us
    ppermute x4, waiting for transfers between devices, _produce_kinds(): ppermute(s_next, along_axis, list(map(lambda p: (p, p ^ a_next), range(fi...  102 us
    dot_general x8, matrix products, contract(): lax.dot_general(left, right, (((left_axis,), (right_axis,)), ((), ())), p...  48.7 us
    reduce_scatter x1, waiting for transfers between devices, on_device(): lax.psum_scatter(grad_out_weight, 'shard', scatter_dimension=0, tiled=True)  32.4 us
  transfers between devices with their start and end apart: 12, of which 8 were waited for; matrix products, arithmetic and copies ran while one was open for 7% of the time, Pallas kernels for 0%

profile of v1, /device:TPU:0, one launch (start us, length us, event | category | flops | bytes accessed | tf_op | source)
XLA Modules:
  0.0 1093.4 jit_solution(9629848327593549295)
XLA Ops:
  13.4 2.9 collective-permute-start.1
  16.3 27.8 %collective-permute-done.1 = bf16[512,1024]{1,0:T(8,128)(2,1)} collective-permute-done((bf16[512,1024]{1,0:T(8,128)(2,1)S(1)}, bf16[512,1024]{1,0:T(8,128)(2,1)}, u32[]{:S(2)}, u32[]{:S(2)}) %collective-permute-start.1) | collective-permute-done | bytes 1048608 | tf_op jit(solution)/shard_map/ppermute | solution.py:19
  44.1 4.0 maximum_select_fusion.2
  50.0 72.0 %collective-permute-done.2 = bf16[1024,1024]{1,0:T(8,128)(2,1)} collective-permute-done((bf16[1024,1024]{1,0:T(8,128)(2,1)S(1)}, bf16[1024,1024]{1,0:T(8,128)(2,1)}, u32[]{:S(2)}, u32[]{:S(2)}) %collective-permute-start.2) | collective-permute-done | bytes 2097184 | tf_op jit(solution)/shard_map/ppermute | solution.py:19
  122.0 4.8 maximum_select_fusion.1
  132.3 239.8 %all-reduce.20 = (bf16[1024]{0:T(1024)(128)(2,1)S(1)}, bf16[1024]{0:T(1024)(128)(2,1)S(1)}, bf16[1024]{0:T(1024)(128)(2,1)S(1)}, bf16[1024]{0:T(1024)(128)(2,1)S...) all-reduce(bf16[1024]{0:T(1024)(128)(2,1)S(1)} %dynamic-update-slic, ...), channel_id=1, replica_groups=mesh['shard'=16,'replica'=2] {'shard'}, use_global_device_ids=true, to_apply=%add.3 | all-reduce | flops 8192 | bytes 32768
  372.2 17.8 %all-gather = bf16[16,1,256]{2,1,0:T(2,128)(2,1)S(1)} all-gather(bf16[1,1,256]{2,1,0:T(2,128)(2,1)S(1)} %reshape.182), channel_id=1, replica_groups=mesh['shard'=16,'replica'=2] {'shard'}, dimensions={0}, use_global_device_ids=true | all-gather | bytes 8704 | tf_op jit(solution)/shard_map/all_gather | solution.py:127
  390.5 3.8 fusion.2
  398.3 4.9 convolution_add_fusion
  403.2 9.6 fusion.60
  412.9 3.0 multiply_reduce_fusion.1
  419.3 3.1 convolution_convert_fusion.1
  429.9 6.8 fusion.32
  438.0 8.2 fusion.22
  448.2 9.1 fusion.39
  457.5 32.4 %reduce-scatter.7.cloned.1.call-done = f32[64,1024]{1,0:T(8,128)} async-done(((f32[1024,1024]{1,0:T(8,128)}), f32[64,1024]{1,0:T(8,128)}) %reduce-scatter.7.cloned.1.call-update) | async-done | bytes 262160 | tf_op jit(solution)/shard_map/reduce_scatter | solution.py:230
  489.9 138.2 %reduce-scatter.5.cloned.1.call-done = f32[64,3072]{1,0:T(8,128)} async-done(((f32[1024,3072]{1,0:T(8,128)}), f32[64,3072]{1,0:T(8,128)}) %reduce-scatter.5.cloned.1.call-update) | async-done | bytes 786448 | tf_op jit(solution)/shard_map/reduce_scatter | solution.py:227
  628.0 182.3 %reduce-scatter.9.cloned.1.call-done = f32[64,4096]{1,0:T(8,128)} async-done(((f32[1024,4096]{1,0:T(8,128)}), f32[64,4096]{1,0:T(8,128)}) %reduce-scatter.9.cloned.1.call-update) | async-done | bytes 1048592 | tf_op jit(solution)/shard_map/reduce_scatter | solution.py:164
  810.3 182.3 %reduce-scatter.11.cloned.1.call-done = f32[256,1024]{1,0:T(8,128)} async-done(((f32[4096,1024]{1,0:T(8,128)}), f32[256,1024]{1,0:T(8,128)}) %reduce-scatter.11.cloned.1.call-update) | async-done | bytes 1048592 | tf_op jit(solution)/shard_map/reduce_scatter | solution.py:166
  994.0 6.0 multiply_reduce_fusion.2
  1000.0 59.6 %all-reduce.17 = (f32[1024]{0:T(1024)S(1)}, f32[1024]{0:T(1024)S(1)}, f32[1024]{0:T(1024)S(1)}, f32[1024]{0:T(1024)S(1)}, f32[1024]{0:T(1024)S(1)}, /*index=5*/f...) all-reduce(f32[1024]{0:T(1024)S(1)} %get-tuple-element.17, ...), channel_id=2, replica_groups=mesh['shard'=16,'replica'=2] {'shard'}, use_global_device_ids=true, to_apply=%region_12.13.clone | all-reduce | flops 12288 | bytes 98304
  1060.4 5.7 all-reduce.18
  1068.3 8.5 fusion.16
  1076.7 4.0 all-reduce.23.cloned.1.call-done
  (152 shorter events, 40.2 us)
Async XLA Ops:
  7.2 383.3 %all-gather.5.cloned.1.call-start = ((), (), s32[]{:S(2)}) async-start(), calls=%async_computation.4 | async-start | bytes 6684672 | tf_op jit(solution)/shard_map/all_gather | solution.py:93
  7.9 387.9 %all-gather.7.cloned.1.call-start = ((), (), s32[]{:S(2)}) async-start(), calls=%async_computation.5 | async-start | bytes 2228224 | tf_op jit(solution)/shard_map/all_gather | solution.py:96
  8.7 389.6 %all-gather.9.cloned.1.call-start = ((), (), s32[]{:S(2)}) async-start(), calls=%async_computation.6 | async-start | bytes 8912896 | tf_op jit(solution)/shard_map/all_gather | solution.py:126
  9.4 480.5 %reduce-scatter.7.cloned.1.call-start = ((), (), s32[]{:S(2)}) async-start(), calls=%async_computation.8 | async-start | bytes 4456448 | tf_op jit(solution)/shard_map/reduce_scatter | solution.py:230
  9.4 2.3 collective-permute-start
  13.4 30.7 %collective-permute-start.1 = (bf16[512,1024]{1,0:T(8,128)(2,1)S(1)}, bf16[512,1024]{1,0:T(8,128)(2,1)}, u32[]{:S(2)}, u32[]{:S(2)}) collective-permute-start(bf16[512,1024]{1,0:T(8,128)(2,1)S(1)} %maximum_select_fusion.9), channel_id=1, source_target_pairs={{0,4},{2,6},{4,0},{6,2},{8,12},{10,14},{12,8},{14,10},{16,20},{18,... | collective-permute-start | bytes 3145736 | tf_op jit(solution)/shard_map/ppermute | solution.py:19
  48.0 74.0 %collective-permute-start.2 = (bf16[1024,1024]{1,0:T(8,128)(2,1)S(1)}, bf16[1024,1024]{1,0:T(8,128)(2,1)}, u32[]{:S(2)}, u32[]{:S(2)}) collective-permute-start(bf16[1024,1024]{1,0:T(8,128)(2,1)S(1)} %maximum_select_fusion.2), channel_id=1, source_target_pairs={{0,8},{2,10},{4,12},{6,14},{8,0},{10,2},{12,4},{14,6},{16,24},{18,... | collective-permute-start | bytes 6291464 | tf_op jit(solution)/shard_map/ppermute | solution.py:19
  49.9 79.3 %copy-start.15 = (u32[32]{0:T(128)S(1)}, u32[32]{0:T(128)}, u32[]{:S(2)}) copy-start(u32[32]{0:T(128)} %constant.50) | copy-start | bytes 388
  49.9 80.6 %copy-start.16 = (bf16[64]{0:T(256)(128)(2,1)S(1)}, bf16[64]{0:T(256)(128)(2,1)}, u32[]{:S(2)}) copy-start(bf16[64]{0:T(256)(128)(2,1)} %param.23) | copy-start | bytes 388
  49.9 80.8 %copy-start.17 = (bf16[64]{0:T(256)(128)(2,1)S(1)}, bf16[64]{0:T(256)(128)(2,1)}, u32[]{:S(2)}) copy-start(bf16[64]{0:T(256)(128)(2,1)} %param.22) | copy-start | bytes 388
  49.9 81.0 %copy-start.18 = (bf16[64]{0:T(256)(128)(2,1)S(1)}, bf16[64]{0:T(256)(128)(2,1)}, u32[]{:S(2)}) copy-start(bf16[64]{0:T(256)(128)(2,1)} %param.20) | copy-start | bytes 388
  49.9 81.3 %copy-start.19 = (bf16[64]{0:T(256)(128)(2,1)S(1)}, bf16[64]{0:T(256)(128)(2,1)}, u32[]{:S(2)}) copy-start(bf16[64]{0:T(256)(128)(2,1)} %param.19) | copy-start | bytes 388
  49.9 81.5 %copy-start.20 = (bf16[64]{0:T(256)(128)(2,1)S(1)}, bf16[64]{0:T(256)(128)(2,1)}, u32[]{:S(2)}) copy-start(bf16[64]{0:T(256)(128)(2,1)} %param.25) | copy-start | bytes 388
  49.9 81.7 %copy-start.21 = (bf16[64]{0:T(256)(128)(2,1)S(1)}, bf16[64]{0:T(256)(128)(2,1)}, u32[]{:S(2)}) copy-start(bf16[64]{0:T(256)(128)(2,1)} %param.31) | copy-start | bytes 388
  49.9 81.9 %copy-start.22 = (bf16[64]{0:T(256)(128)(2,1)S(1)}, bf16[64]{0:T(256)(128)(2,1)}, u32[]{:S(2)}) copy-start(bf16[64]{0:T(256)(128)(2,1)} %param.27) | copy-start | bytes 388
  49.9 82.2 %copy-start.23 = (bf16[64]{0:T(256)(128)(2,1)S(1)}, bf16[64]{0:T(256)(128)(2,1)}, u32[]{:S(2)}) copy-start(bf16[64]{0:T(256)(128)(2,1)} %param.26) | copy-start | bytes 388
  50.0 322.2 %copy-start.24 = (bf16[256]{0:T(256)(128)(2,1)S(1)}, bf16[256]{0:T(256)(128)(2,1)}, u32[]{:S(2)}) copy-start(bf16[256]{0:T(256)(128)(2,1)} %param.29) | copy-start | bytes 1540
  50.0 340.0 %copy-start = (f32[128,1024]{1,0:T(8,128)S(1)}, f32[128,1024]{1,0:T(8,128)}, u32[]{:S(2)}) copy-start(f32[128,1024]{1,0:T(8,128)} %param.16) | copy-start | bytes 1572868
  50.0 340.4 %copy-start.14 = (s32[1,128]{1,0:T(1,128)S(1)}, s32[1,128]{1,0:T(1,128)}, u32[]{:S(2)}) copy-start(s32[1,128]{1,0:T(1,128)} %param.17) | copy-start | bytes 1540
  126.8 276.4 %collective-permute-start.3 = (bf16[2048,1024]{1,0:T(8,128)(2,1)}, bf16[2048,1024]{1,0:T(8,128)(2,1)}, u32[]{:S(2)}, u32[]{:S(2)}) collective-permute-start(bf16[2048,1024]{1,0:T(8,128)(2,1)} %maximum_select_fusion.1), channel_id=1, source_target_pairs={{0,16},{2,18},{4,20},{6,22},{8,24},{10,26},{12,28},{14,30},{16,0},... | collective-permute-start | bytes 12582920 | tf_op jit(solution)/shard_map/ppermute | solution.py:19
  419.0 209.0 %reduce-scatter.5.cloned.1.call-start = ((), (), s32[]{:S(2)}) async-start(), calls=%async_computation.7 | async-start | bytes 13369344 | tf_op jit(solution)/shard_map/reduce_scatter | solution.py:227
  436.8 373.5 %reduce-scatter.9.cloned.1.call-start = ((), (), s32[]{:S(2)}) async-start(), calls=%async_computation.9 | async-start | bytes 17825792 | tf_op jit(solution)/shard_map/reduce_scatter | solution.py:164
  446.2 546.4 %reduce-scatter.11.cloned.1.call-start = ((), (), s32[]{:S(2)}) async-start(), calls=%async_computation.10 | async-start | bytes 17825792 | tf_op jit(solution)/shard_map/reduce_scatter | solution.py:166
  457.4 623.3 %all-reduce.23.cloned.1.call-start = ((), (), s32[]{:S(2)}) async-start(), calls=%async_computation.11 | async-start | bytes 6291456 | tf_op jit(solution)/shard_map/psum | solution.py:241
  (15 other events, 84.1 us)
Sparse Core Ops, SparseCore 0:
  10.3 81.6 all-gather.4
  94.1 137.8 all-gather.6
  234.2 146.5 all-gather.8
  419.1 70.7 reduce-scatter.6
  494.3 133.6 reduce-scatter.4
  632.6 177.6 reduce-scatter.8
  815.0 177.5 reduce-scatter.10
  995.2 85.4 all-reduce.22
